TPU v7x, 512 devices: a whole 4x4x16 slice. The times are simulated.
512 devices in a mesh: mp: 2 (over y_hi), tok: 8 (over x, core), lat: 32 (over z, y_lo).
Axes of the slice: x: 4, y: 4 (y_hi: 2, y_lo: 2; y = y_hi * 2 + y_lo), z: 16, core: 2. Of those that a mesh axis runs over, the one named last changes fastest.
Arguments:
- inputs: bfloat16 [2, 384, 4608], P('mp', 'lat', 'tok'), may hold values from -6 to 6
- gate_w: bfloat16 [2, 4608, 18432], P('mp', 'tok', 'lat'), may hold values from -0.09375 to 0.09375
- up_w: bfloat16 [2, 4608, 18432], P('mp', 'tok', 'lat'), may hold values from -0.09375 to 0.09375
- down_w: bfloat16 [2, 18432, 4608], P('mp', 'lat', 'tok'), may hold values from -0.046875 to 0.046875
- enc_w: bfloat16 [2, 4608, 8192], P('mp', 'tok', 'lat'), may hold values from -0.0625 to 0.0625
- enc_bias: float32 [8192], P('lat'), may hold values from -3 to 3
- dec_w: bfloat16 [8192, 2, 4608], P('lat', 'mp', 'tok'), may hold values from -0.0625 to 0.0625
- dec_bias: float32 [2, 4608], P('mp', 'tok'), may hold values from -3 to 3
Outputs:
- recon_error: float32 [2, 384, 4608], P('mp', 'lat', 'tok')
- dec_grad: float32 [8192, 2, 4608], P('lat', 'mp', 'tok')
- latent_grad: float32 [384, 8192], P(None, 'lat')
All inputs are finite; a program needn't handle non-finite values.
Results may differ from a plain program's by a relative error of at most 0.009.
Values may be sent and summed in bfloat16 or wider, within the bound.
A program may use at most 64 MiB of HBM per device.

v0:
```python
import jax
import jax.numpy as jnp
from jax import lax
from jax.sharding import PartitionSpec as P


def contract_rows(left, right):
    return lax.dot_general(
        left, right, (((0,), (0,)), ((), ())), preferred_element_type=jnp.float32
    )


def contract_cols(left, right):
    return lax.dot_general(
        left, right, (((1,), (1,)), ((), ())), preferred_element_type=jnp.float32
    )


def body(inputs, gate_w, up_w, down_w, enc_w, enc_bias, dec_w, dec_bias):
    x_rows = inputs[0]
    gathered = lax.all_gather(x_rows, "lat", axis=0, tiled=True)
    gate_local = gate_w[0]
    up_local = up_w[0]
    width = gate_local.shape[1]
    block = gathered
    both = lax.psum_scatter(
        jnp.concatenate(
            [
                jnp.dot(block, gate_local, preferred_element_type=jnp.float32),
                jnp.dot(block, up_local, preferred_element_type=jnp.float32),
            ],
            axis=1,
        ),
        "tok",
        scatter_dimension=0,
        tiled=True,
    )
    hidden = (jax.nn.gelu(both[:, :width], approximate=True) * both[:, width:]).astype(jnp.bfloat16)
    hidden_all = lax.all_gather(hidden, "tok", axis=0, tiled=True)
    down_local = down_w[0]
    block = hidden_all
    acts = lax.psum_scatter(
        jnp.dot(block, down_local, preferred_element_type=jnp.float32),
        "lat",
        scatter_dimension=0,
        tiled=True,
    ).astype(jnp.bfloat16)
    acts_all = lax.all_gather(acts, "lat", axis=0, tiled=True)
    partial_pre = jnp.dot(acts_all, enc_w[0], preferred_element_type=jnp.float32)
    pre = lax.psum(partial_pre, ("mp", "tok"))
    codes = jnp.maximum(pre + enc_bias, 0.0).astype(jnp.bfloat16)
    decoder = dec_w[:, 0, :]
    bias_row = dec_bias[0]
    block = codes
    recon = lax.psum_scatter(
        jnp.dot(block, decoder, preferred_element_type=jnp.float32),
        "lat",
        scatter_dimension=0,
        tiled=True,
    )
    error = recon + bias_row - acts.astype(jnp.float32)
    error_all = lax.all_gather(error.astype(jnp.bfloat16), "lat", axis=0, tiled=True)
    decoder_grad = contract_rows(codes, error_all)
    latent_grad = lax.psum(contract_cols(error_all, decoder), ("mp", "tok"))
    return (error[None], decoder_grad[:, None, :], latent_grad)


def solution(mesh):
    in_specs = (
        P("mp", "lat", "tok"),
        P("mp", "tok", "lat"),
        P("mp", "tok", "lat"),
        P("mp", "lat", "tok"),
        P("mp", "tok", "lat"),
        P("lat"),
        P("lat", "mp", "tok"),
        P("mp", "tok"),
    )
    out_specs = (P("mp", "lat", "tok"), P("lat", "mp", "tok"), P(None, "lat"))
    return jax.shard_map(body, mesh=mesh, in_specs=in_specs, out_specs=out_specs, check_vma=False)
```

profile of v0, /device:TPU:1, one launch (start us, length us, event | category | flops | bytes accessed | tf_op | source)
XLA Modules:
  0.0 789.7 jit_solution(4947730989583786598)
XLA Ops:
  7.2 0.0 reduce-scatter.8.cloned.1.call-start
  7.2 0.8 copy.20
  8.0 61.9 %all-gather = bf16[1,384,576]{2,0,1:T(2,128)(2,1)S(1)} all-gather(bf16[1,12,576]{2,0,1:T(2,128)(2,1)S(1)} %copy.20), channel_id=2, replica_groups=mesh['mp'=2,'tok'=8,'lat'=32] {'lat'}, dimensions={1}, use_global_device_ids=true | all-gather | bytes 456192 | tf_op jit(solution)/shard_map/all_gather | solution.py:21
  70.0 0.7 copy.21
  70.6 0.6 fusion.4
  71.3 0.6 fusion.6
  71.9 0.1 pad_maximum_fusion
  72.1 2.0 copy.25
  74.1 0.0 all-reduce.7.cloned.1.call-start
  74.1 47.7 %reduce-scatter.8.cloned.1.call-done = f32[48,1152]{1,0:T(8,128)} async-done(((f32[384,1152]{1,0:T(8,128)}), f32[48,1152]{1,0:T(8,128)}) %reduce-scatter.8.cloned.1.call-update) | async-done | bytes 221200 | tf_op jit(solution)/shard_map/reduce_scatter | solution.py:26
  121.8 1.1 fusion.24
  122.9 15.4 %all_gather.13 = bf16[384,576]{1,0:T(8,128)(2,1)S(1)} all-gather(bf16[48,576]{1,0:T(8,128)(2,1)S(1)} %fusion.24), channel_id=1, replica_groups=mesh['mp'=2,'tok'=8,'lat'=32] {'tok'}, dimensions={0}, use_global_device_ids=true | all-gather | bytes 497664 | tf_op jit(solution)/shard_map/all_gather | solution.py:39
  138.2 0.6 fusion.2
  138.8 59.0 %fusion = f32[16,576]{1,0:T(8,128)S(1)} fusion(f32[384,576]{1,0:T(8,128)S(1)} %fusion.2), kind=kCustom, calls=%all-reduce-scatter | all-reduce-scatter fusion | flops 294913 | bytes 923648
  197.9 1.7 collective-permute-start
  199.6 2.1 collective-permute-start.1
  201.7 6.0 collective-permute-start.7
  207.7 4.9 collective-permute-start.2
  212.7 4.9 collective-permute-start.3
  217.6 2.1 collective-permute-start.4
  219.8 3.5 collective-permute-start.5
  223.2 2.8 collective-permute-start.6
  226.1 1.3 dynamic-slice.6
  228.1 1.3 concatenate.4
  229.4 49.4 %all-gather.1 = bf16[32,12,576]{2,1,0:T(8,128)(2,1)S(1)} all-gather(bf16[1,12,576]{2,1,0:T(8,128)(2,1)S(1)} %fusion.31), channel_id=1, replica_groups=mesh['mp'=2,'tok'=8,'lat'=32] {'lat'}, dimensions={0}, use_global_device_ids=true | all-gather | bytes 456192 | tf_op jit(solution)/shard_map/all_gather | solution.py:48
  278.8 0.2 reshape.9
  279.1 1.1 fusion.14
  280.2 0.0 all-reduce.9.cloned.1.call-start
  280.2 180.0 %all-reduce.7.cloned.1.call-done = f32[384,256]{1,0:T(8,128)} async-done(((f32[384,256]{1,0:T(8,128)}), f32[384,256]{1,0:T(8,128)}) %all-reduce.7.cloned.1.call-update) | async-done | bytes 393232 | tf_op jit(solution)/shard_map/psum | solution.py:50
  460.2 1.3 fusion.12
  461.6 59.2 %fusion.1 = f32[16,576]{1,0:T(8,128)S(1)} fusion(f32[384,576]{1,0:T(8,128)S(1)} %fusion.12), kind=kCustom, calls=%all-reduce-scatter.1 | all-reduce-scatter fusion | flops 294913 | bytes 923648
  520.7 1.3 collective-permute-start.10
  522.0 3.4 collective-permute-start.11
  525.5 7.0 collective-permute-start.15
  532.6 4.5 collective-permute-start.12
  537.1 3.9 collective-permute-start.13
  541.0 2.9 collective-permute-start.14
  543.9 3.1 collective-permute-start.8
  547.0 2.2 collective-permute-start.9
  549.3 1.0 collective-permute-done.9
  550.3 1.0 concatenate.5
  551.3 48.9 %all-gather.2 = bf16[32,12,576]{2,1,0:T(8,128)(2,1)S(1)} all-gather(bf16[1,12,576]{2,1,0:T(8,128)(2,1)S(1)} %get-tuple-element.18), channel_id=1, replica_groups=mesh['mp'=2,'tok'=8,'lat'=32] {'lat'}, dimensions={0}, use_global_device_ids=true | all-gather | bytes 456192 | tf_op jit(solution)/shard_map/all_gather | solution.py:62
  600.2 0.2 reshape.11
  600.4 1.1 fusion.10
  601.5 0.6 copy.24
  602.2 1.2 convolution_bitcast_fusion
  603.3 178.1 %all-reduce.9.cloned.1.call-done = f32[384,256]{1,0:T(8,128)} async-done(((f32[384,256]{1,0:T(8,128)}), f32[384,256]{1,0:T(8,128)}) %all-reduce.9.cloned.1.call-update) | async-done | bytes 393232 | tf_op jit(solution)/shard_map/psum | solution.py:64
  781.4 1.8 copy.29
  (40 shorter events, 0.2 us)
Async XLA Ops:
  7.2 63.5 %copy-start = (bf16[1,576,576]{2,1,0:T(8,128)(2,1)S(1)}, bf16[1,576,576]{2,1,0:T(8,128)(2,1)}, u32[]{:S(2)}) copy-start(bf16[1,576,576]{2,1,0:T(8,128)(2,1)} %param.10) | copy-start | bytes 1990660
  7.2 114.6 %reduce-scatter.8.cloned.1.call-start = ((), (), s32[]{:S(2)}) async-start(), calls=%async_computation.3 | async-start | bytes 1990656 | tf_op jit(solution)/shard_map/reduce_scatter | solution.py:26
  70.0 1.3 copy-start.3
  74.0 64.2 %copy-start.4 = (bf16[1,576,576]{2,1,0:T(8,128)(2,1)S(1)}, bf16[1,576,576]{2,1,0:T(8,128)(2,1)}, u32[]{:S(2)}) copy-start(bf16[1,576,576]{2,1,0:T(8,128)(2,1)} %param.11) | copy-start | bytes 1990660
  74.1 386.2 %all-reduce.7.cloned.1.call-start = ((), (), s32[]{:S(2)}) async-start(), calls=%async_computation.1 | async-start | bytes 786432 | tf_op jit(solution)/shard_map/psum | solution.py:50
  138.8 140.3 %copy-start.5 = (bf16[1,576,256]{2,1,0:T(8,128)(2,1)S(1)}, bf16[1,576,256]{2,1,0:T(8,128)(2,1)}, u32[]{:S(2)}) copy-start(bf16[1,576,256]{2,1,0:T(8,128)(2,1)} %param.12) | copy-start | bytes 884740
  197.9 21.9 %collective-permute-start = (bf16[16,576]{1,0:T(8,128)(2,1)S(1)}, bf16[16,576]{1,0:T(8,128)(2,1)S(1)}, u32[]{:S(2)}, u32[]{:S(2)}) collective-permute-start(bf16[16,576]{1,0:T(8,128)(2,1)S(1)} %convert.14), channel_id=1, source_target_pairs={{0,1},{1,2},{2,3},{3,4},{4,5},{5,6},{6,7},{7,8},{8,9},{9,10},{10,1... | collective-permute-start | bytes 55304
  199.6 23.6 %collective-permute-start.1 = (bf16[16,576]{1,0:T(8,128)(2,1)S(1)}, bf16[16,576]{1,0:T(8,128)(2,1)S(1)}, u32[]{:S(2)}, u32[]{:S(2)}) collective-permute-start(bf16[16,576]{1,0:T(8,128)(2,1)S(1)} %convert.14), channel_id=1, source_target_pairs={{0,2},{1,3},{2,4},{3,5},{4,6},{5,7},{6,8},{7,9},{8,10},{9,11},{10,... | collective-permute-start | bytes 55304
  201.7 15.9 %collective-permute-start.7 = (bf16[12,576]{1,0:T(8,128)(2,1)S(1)}, bf16[12,576]{1,0:T(8,128)(2,1)S(1)}, u32[]{:S(2)}, u32[]{:S(2)}) collective-permute-start(bf16[12,576]{1,0:T(8,128)(2,1)S(1)} %slice.10), channel_id=1, source_target_pairs={{0,8},{1,9},{2,10},{3,11},{4,12},{5,13},{6,14},{7,15},{8,16},{9,17... | collective-permute-start | bytes 41480
  207.7 20.3 %collective-permute-start.2 = (bf16[16,576]{1,0:T(8,128)(2,1)S(1)}, bf16[16,576]{1,0:T(8,128)(2,1)S(1)}, u32[]{:S(2)}, u32[]{:S(2)}) collective-permute-start(bf16[16,576]{1,0:T(8,128)(2,1)S(1)} %convert.14), channel_id=1, source_target_pairs={{0,3},{1,4},{2,5},{3,6},{4,7},{5,8},{6,9},{7,10},{8,11},{9,12},{10... | collective-permute-start | bytes 55304
  212.7 15.3 %collective-permute-start.3 = (bf16[16,576]{1,0:T(8,128)(2,1)S(1)}, bf16[16,576]{1,0:T(8,128)(2,1)S(1)}, u32[]{:S(2)}, u32[]{:S(2)}) collective-permute-start(bf16[16,576]{1,0:T(8,128)(2,1)S(1)} %convert.14), channel_id=1, source_target_pairs={{0,4},{1,5},{2,6},{3,7},{4,8},{5,9},{6,10},{7,11},{8,12},{9,13},{1... | collective-permute-start | bytes 55304
  217.6 10.4 %collective-permute-start.4 = (bf16[16,576]{1,0:T(8,128)(2,1)S(1)}, bf16[16,576]{1,0:T(8,128)(2,1)S(1)}, u32[]{:S(2)}, u32[]{:S(2)}) collective-permute-start(bf16[16,576]{1,0:T(8,128)(2,1)S(1)} %convert.14), channel_id=1, source_target_pairs={{0,5},{1,6},{2,7},{3,8},{4,9},{5,10},{6,11},{7,12},{8,13},{9,14},{... | collective-permute-start | bytes 55304
  219.8 8.3 %collective-permute-start.5 = (bf16[16,576]{1,0:T(8,128)(2,1)S(1)}, bf16[16,576]{1,0:T(8,128)(2,1)S(1)}, u32[]{:S(2)}, u32[]{:S(2)}) collective-permute-start(bf16[16,576]{1,0:T(8,128)(2,1)S(1)} %convert.14), channel_id=1, source_target_pairs={{0,6},{1,7},{2,8},{3,9},{4,10},{5,11},{6,12},{7,13},{8,14},{9,15},... | collective-permute-start | bytes 55304
  223.2 4.8 collective-permute-start.6
  229.4 230.8 %copy-start.2 = (bf16[256,1,576]{0,2,1:T(8,128)(2,1)S(1)}, bf16[256,1,576]{0,2,1:T(8,128)(2,1)}, u32[]{:S(2)}) copy-start(bf16[256,1,576]{0,2,1:T(8,128)(2,1)} %param.14) | copy-start | bytes 884740
  229.4 230.8 %copy-start.6 = (f32[256]{0:T(256)S(1)}, f32[256]{0:T(256)}, u32[]{:S(2)}) copy-start(f32[256]{0:T(256)} %param.13) | copy-start | bytes 3076
  280.2 269.0 %copy-start.7 = (f32[1,576]{1,0:T(1,128)S(1)}, f32[1,576]{1,0:T(1,128)}, u32[]{:S(2)}) copy-start(f32[1,576]{1,0:T(1,128)} %param.15) | copy-start | bytes 6916
  280.2 501.2 %all-reduce.9.cloned.1.call-start = ((), (), s32[]{:S(2)}) async-start(), calls=%async_computation.2 | async-start | bytes 786432 | tf_op jit(solution)/shard_map/psum | solution.py:64
  520.7 23.1 %collective-permute-start.10 = (f32[16,576]{1,0:T(8,128)S(1)}, f32[16,576]{1,0:T(8,128)S(1)}, u32[]{:S(2)}, u32[]{:S(2)}) collective-permute-start(f32[16,576]{1,0:T(8,128)S(1)} %fusion.1), channel_id=1, source_target_pairs={{0,3},{1,4},{2,5},{3,6},{4,7},{5,8},{6,9},{7,10},{8,11},{9,12},{10... | collective-permute-start | bytes 110600
  522.0 24.9 %collective-permute-start.11 = (f32[16,576]{1,0:T(8,128)S(1)}, f32[16,576]{1,0:T(8,128)S(1)}, u32[]{:S(2)}, u32[]{:S(2)}) collective-permute-start(f32[16,576]{1,0:T(8,128)S(1)} %fusion.1), channel_id=1, source_target_pairs={{0,4},{1,5},{2,6},{3,7},{4,8},{5,9},{6,10},{7,11},{8,12},{9,13},{1... | collective-permute-start | bytes 110600
  525.5 15.5 %collective-permute-start.15 = (f32[12,576]{1,0:T(8,128)S(1)}, f32[12,576]{1,0:T(8,128)S(1)}, u32[]{:S(2)}, u32[]{:S(2)}) collective-permute-start(f32[12,576]{1,0:T(8,128)S(1)} %slice.11), channel_id=1, source_target_pairs={{0,8},{1,9},{2,10},{3,11},{4,12},{5,13},{6,14},{7,15},{8,16},{9,17... | collective-permute-start | bytes 82952
  532.6 16.7 %collective-permute-start.12 = (f32[16,576]{1,0:T(8,128)S(1)}, f32[16,576]{1,0:T(8,128)S(1)}, u32[]{:S(2)}, u32[]{:S(2)}) collective-permute-start(f32[16,576]{1,0:T(8,128)S(1)} %fusion.1), channel_id=1, source_target_pairs={{0,5},{1,6},{2,7},{3,8},{4,9},{5,10},{6,11},{7,12},{8,13},{9,14},{... | collective-permute-start | bytes 110600
  537.1 12.2 %collective-permute-start.13 = (f32[16,576]{1,0:T(8,128)S(1)}, f32[16,576]{1,0:T(8,128)S(1)}, u32[]{:S(2)}, u32[]{:S(2)}) collective-permute-start(f32[16,576]{1,0:T(8,128)S(1)} %fusion.1), channel_id=1, source_target_pairs={{0,6},{1,7},{2,8},{3,9},{4,10},{5,11},{6,12},{7,13},{8,14},{9,15},... | collective-permute-start | bytes 110600
  541.0 8.2 %collective-permute-start.14 = (f32[16,576]{1,0:T(8,128)S(1)}, f32[16,576]{1,0:T(8,128)S(1)}, u32[]{:S(2)}, u32[]{:S(2)}) collective-permute-start(f32[16,576]{1,0:T(8,128)S(1)} %fusion.1), channel_id=1, source_target_pairs={{0,7},{1,8},{2,9},{3,10},{4,11},{5,12},{6,13},{7,14},{8,15},{9,16}... | collective-permute-start | bytes 110600
  543.9 5.4 collective-permute-start.8
  547.0 3.3 collective-permute-start.9
  551.3 50.8 %copy-start.1 = (f32[384,256]{1,0:T(8,128)S(1)}, f32[384,256]{1,0:T(8,128)}, u32[]{:S(2)}) copy-start(f32[384,256]{1,0:T(8,128)} %all-reduce.7.cloned.1.call-done) | copy-start | bytes 1179652
Sparse Core Ops, SparseCore 0:
  74.2 47.5 reduce-scatter.7
  280.3 179.8 all-reduce.6
  601.6 179.7 all-reduce.8
where the time goes:
time: 790 us
  waiting for transfers between devices  407 us (52%)
  blocking collectives  294 us (37%)
  starting transfers between devices  56.6 us (7%)
  between operations  14.9 us (2%)
  local copies, waits for them, and re-layouts  10 us (1%)
    psum x1, waiting for transfers between devices, body(): pre = lax.psum(partial_pre, ('mp', 'tok'))  180 us
    psum x1, waiting for transfers between devices, body(): latent_grad = lax.psum(contract_cols(error_all, decoder), ('mp', 'tok'))  178 us
    unnamed x2, blocking collectives  118 us
    all_gather x1, blocking collectives, body(): gathered = lax.all_gather(x_rows, 'lat', axis=0, tiled=True)  61.9 us
    unnamed x16, starting transfers between devices  56.5 us
    all_gather x1, blocking collectives, body(): acts_all = lax.all_gather(acts, 'lat', axis=0, tiled=True)  49.4 us
    all_gather x1, blocking collectives, body(): lax.all_gather(error.astype(jnp.bfloat16), 'lat', axis=0, tiled=True)  48.9 us
    reduce_scatter x1, waiting for transfers between devices, body(): lax.psum_scatter(jnp.concatenate([jnp.dot(block, gate_local, preferred_el...  47.7 us
  transfers between devices with their start and end apart: 19, of which 4 were waited for; matrix products, arithmetic and copies ran while one was open for 0% of the time, Pallas kernels for 0%

commit v1 on v0

--- a/solution.py
+++ b/solution.py
@@ -61,7 +61,7 @@
     error = recon + bias_row - acts.astype(jnp.float32)
     error_all = lax.all_gather(error.astype(jnp.bfloat16), "lat", axis=0, tiled=True)
     decoder_grad = contract_rows(codes, error_all)
-    latent_grad = lax.psum(contract_cols(error_all, decoder), ("mp", "tok"))
+    latent_grad = lax.psum(lax.psum(contract_cols(error_all, decoder), "mp"), "tok")
     return (error[None], decoder_grad[:, None, :], latent_grad)
 
 

time: 790 us -> 763 us (0.966)
  waiting for transfers between devices: 407 us -> 378 us
    psum x1 -> x2, waiting for transfers between devices: 178 us -> 150 us  [the longest x1 75.6 us: body(): lax.psum(contract_cols(error_all, decoder), 'mp')]
  transfers between devices with their start and end apart: 19 -> 20, of which waited for: 4 -> 5; matrix products, arithmetic and copies ran while one was open for 0% -> 0% of each run, Pallas kernels for 0% -> 0%
where the time goes in v1:
time: 763 us; the launch traced here: 761 us
  waiting for transfers between devices  378 us (50%)
  blocking collectives  294 us (39%)
  starting transfers between devices  56.6 us (7%)
  between operations  14.9 us (2%)
  local copies, waits for them, and re-layouts  10 us (1%)
    psum x1, waiting for transfers between devices, body(): pre = lax.psum(partial_pre, ('mp', 'tok'))  180 us
    unnamed x2, blocking collectives  118 us
    psum x1, waiting for transfers between devices, body(): lax.psum(contract_cols(error_all, decoder), 'mp')  75.6 us
    psum x1, waiting for transfers between devices, body(): lax.psum(lax.psum(contract_cols(error_all, decoder), 'mp'), 'tok')  74.1 us
    all_gather x1, blocking collectives, body(): gathered = lax.all_gather(x_rows, 'lat', axis=0, tiled=True)  61.9 us
    unnamed x16, starting transfers between devices  56.5 us
    all_gather x1, blocking collectives, body(): acts_all = lax.all_gather(acts, 'lat', axis=0, tiled=True)  49.4 us
    all_gather x1, blocking collectives, body(): lax.all_gather(error.astype(jnp.bfloat16), 'lat', axis=0, tiled=True)  48.9 us
  transfers between devices with their start and end apart: 20, of which 5 were waited for; matrix products, arithmetic and copies ran while one was open for 0% of the time, Pallas kernels for 0%

profile of v1, /device:TPU:1, one launch (start us, length us, event | category | flops | bytes accessed | tf_op | source)
XLA Modules:
  0.0 761.4 jit_solution(12192304775920358979)
XLA Ops:
  7.2 0.8 copy.20
  8.0 61.9 %all-gather = bf16[1,384,576]{2,0,1:T(2,128)(2,1)S(1)} all-gather(bf16[1,12,576]{2,0,1:T(2,128)(2,1)S(1)} %copy.20), channel_id=2, replica_groups=mesh['mp'=2,'tok'=8,'lat'=32] {'lat'}, dimensions={1}, use_global_device_ids=true | all-gather | bytes 456192 | tf_op jit(solution)/shard_map/all_gather | solution.py:21
  70.0 0.7 copy.21
  70.6 0.6 fusion.4
  71.3 0.6 fusion.6
  71.9 0.1 pad_maximum_fusion
  72.1 2.0 copy.25
  74.1 0.0 all-reduce.8.cloned.1.call-start
  74.1 47.7 %reduce-scatter.8.cloned.1.call-done = f32[48,1152]{1,0:T(8,128)} async-done(((f32[384,1152]{1,0:T(8,128)}), f32[48,1152]{1,0:T(8,128)}) %reduce-scatter.8.cloned.1.call-update) | async-done | bytes 221200 | tf_op jit(solution)/shard_map/reduce_scatter | solution.py:26
  121.8 1.1 fusion.24
  122.9 15.4 %all_gather.13 = bf16[384,576]{1,0:T(8,128)(2,1)S(1)} all-gather(bf16[48,576]{1,0:T(8,128)(2,1)S(1)} %fusion.24), channel_id=1, replica_groups=mesh['mp'=2,'tok'=8,'lat'=32] {'tok'}, dimensions={0}, use_global_device_ids=true | all-gather | bytes 497664 | tf_op jit(solution)/shard_map/all_gather | solution.py:39
  138.2 0.6 fusion.2
  138.8 59.0 %fusion = f32[16,576]{1,0:T(8,128)S(1)} fusion(f32[384,576]{1,0:T(8,128)S(1)} %fusion.2), kind=kCustom, calls=%all-reduce-scatter | all-reduce-scatter fusion | flops 294913 | bytes 923648
  197.9 1.7 collective-permute-start
  199.6 2.1 collective-permute-start.1
  201.7 6.0 collective-permute-start.7
  207.7 4.9 collective-permute-start.2
  212.7 4.9 collective-permute-start.3
  217.6 2.1 collective-permute-start.4
  219.8 3.5 collective-permute-start.5
  223.2 2.8 collective-permute-start.6
  226.1 1.3 dynamic-slice.6
  228.1 1.3 concatenate.4
  229.4 49.4 %all-gather.1 = bf16[32,12,576]{2,1,0:T(8,128)(2,1)S(1)} all-gather(bf16[1,12,576]{2,1,0:T(8,128)(2,1)S(1)} %fusion.31), channel_id=1, replica_groups=mesh['mp'=2,'tok'=8,'lat'=32] {'lat'}, dimensions={0}, use_global_device_ids=true | all-gather | bytes 456192 | tf_op jit(solution)/shard_map/all_gather | solution.py:48
  278.8 0.2 reshape.9
  279.1 1.1 fusion.14
  280.2 180.0 %all-reduce.8.cloned.1.call-done = f32[384,256]{1,0:T(8,128)} async-done(((f32[384,256]{1,0:T(8,128)}), f32[384,256]{1,0:T(8,128)}) %all-reduce.8.cloned.1.call-update) | async-done | bytes 393232 | tf_op jit(solution)/shard_map/psum | solution.py:50
  460.2 1.3 fusion.12
  461.6 59.2 %fusion.1 = f32[16,576]{1,0:T(8,128)S(1)} fusion(f32[384,576]{1,0:T(8,128)S(1)} %fusion.12), kind=kCustom, calls=%all-reduce-scatter.1 | all-reduce-scatter fusion | flops 294913 | bytes 923648
  520.7 1.3 collective-permute-start.10
  522.0 3.4 collective-permute-start.11
  525.5 7.0 collective-permute-start.15
  532.6 4.5 collective-permute-start.12
  537.1 3.9 collective-permute-start.13
  541.0 2.9 collective-permute-start.14
  543.9 3.1 collective-permute-start.8
  547.0 2.2 collective-permute-start.9
  549.3 1.0 collective-permute-done.9
  550.3 1.0 concatenate.5
  551.3 48.9 %all-gather.2 = bf16[32,12,576]{2,1,0:T(8,128)(2,1)S(1)} all-gather(bf16[1,12,576]{2,1,0:T(8,128)(2,1)S(1)} %get-tuple-element.18), channel_id=1, replica_groups=mesh['mp'=2,'tok'=8,'lat'=32] {'lat'}, dimensions={0}, use_global_device_ids=true | all-gather | bytes 456192 | tf_op jit(solution)/shard_map/all_gather | solution.py:62
  600.2 0.2 reshape.11
  600.4 1.1 fusion.10
  601.5 0.0 all-reduce.12.cloned.1.call-start
  601.6 75.6 %all-reduce.10.cloned.1.call-done = f32[384,256]{1,0:T(8,128)} async-done(((f32[384,256]{1,0:T(8,128)}), f32[384,256]{1,0:T(8,128)}) %all-reduce.10.cloned.1.call-update) | async-done | bytes 393232 | tf_op jit(solution)/shard_map/psum | solution.py:64
  677.2 0.6 copy.24
  677.8 1.2 convolution_bitcast_fusion
  679.0 74.1 %all-reduce.12.cloned.1.call-done = f32[384,256]{1,0:T(8,128)} async-done(((f32[384,256]{1,0:T(8,128)}), f32[384,256]{1,0:T(8,128)}) %all-reduce.12.cloned.1.call-update) | async-done | bytes 393232 | tf_op jit(solution)/shard_map/psum | solution.py:64
  753.1 1.8 copy.30
  (43 shorter events, 0.3 us)
Async XLA Ops:
  7.2 63.5 %copy-start = (bf16[1,576,576]{2,1,0:T(8,128)(2,1)S(1)}, bf16[1,576,576]{2,1,0:T(8,128)(2,1)}, u32[]{:S(2)}) copy-start(bf16[1,576,576]{2,1,0:T(8,128)(2,1)} %param.10) | copy-start | bytes 1990660
  7.2 114.6 %reduce-scatter.8.cloned.1.call-start = ((), (), s32[]{:S(2)}) async-start(), calls=%async_computation.4 | async-start | bytes 1990656 | tf_op jit(solution)/shard_map/reduce_scatter | solution.py:26
  70.0 1.3 copy-start.3
  74.0 64.2 %copy-start.4 = (bf16[1,576,576]{2,1,0:T(8,128)(2,1)S(1)}, bf16[1,576,576]{2,1,0:T(8,128)(2,1)}, u32[]{:S(2)}) copy-start(bf16[1,576,576]{2,1,0:T(8,128)(2,1)} %param.11) | copy-start | bytes 1990660
  74.1 386.2 %all-reduce.8.cloned.1.call-start = ((), (), s32[]{:S(2)}) async-start(), calls=%async_computation.1 | async-start | bytes 786432 | tf_op jit(solution)/shard_map/psum | solution.py:50
  138.8 140.3 %copy-start.5 = (bf16[1,576,256]{2,1,0:T(8,128)(2,1)S(1)}, bf16[1,576,256]{2,1,0:T(8,128)(2,1)}, u32[]{:S(2)}) copy-start(bf16[1,576,256]{2,1,0:T(8,128)(2,1)} %param.12) | copy-start | bytes 884740
  197.9 21.9 %collective-permute-start = (bf16[16,576]{1,0:T(8,128)(2,1)S(1)}, bf16[16,576]{1,0:T(8,128)(2,1)S(1)}, u32[]{:S(2)}, u32[]{:S(2)}) collective-permute-start(bf16[16,576]{1,0:T(8,128)(2,1)S(1)} %convert.14), channel_id=1, source_target_pairs={{0,1},{1,2},{2,3},{3,4},{4,5},{5,6},{6,7},{7,8},{8,9},{9,10},{10,1... | collective-permute-start | bytes 55304
  199.6 23.6 %collective-permute-start.1 = (bf16[16,576]{1,0:T(8,128)(2,1)S(1)}, bf16[16,576]{1,0:T(8,128)(2,1)S(1)}, u32[]{:S(2)}, u32[]{:S(2)}) collective-permute-start(bf16[16,576]{1,0:T(8,128)(2,1)S(1)} %convert.14), channel_id=1, source_target_pairs={{0,2},{1,3},{2,4},{3,5},{4,6},{5,7},{6,8},{7,9},{8,10},{9,11},{10,... | collective-permute-start | bytes 55304
  201.7 15.9 %collective-permute-start.7 = (bf16[12,576]{1,0:T(8,128)(2,1)S(1)}, bf16[12,576]{1,0:T(8,128)(2,1)S(1)}, u32[]{:S(2)}, u32[]{:S(2)}) collective-permute-start(bf16[12,576]{1,0:T(8,128)(2,1)S(1)} %slice.10), channel_id=1, source_target_pairs={{0,8},{1,9},{2,10},{3,11},{4,12},{5,13},{6,14},{7,15},{8,16},{9,17... | collective-permute-start | bytes 41480
  207.7 20.3 %collective-permute-start.2 = (bf16[16,576]{1,0:T(8,128)(2,1)S(1)}, bf16[16,576]{1,0:T(8,128)(2,1)S(1)}, u32[]{:S(2)}, u32[]{:S(2)}) collective-permute-start(bf16[16,576]{1,0:T(8,128)(2,1)S(1)} %convert.14), channel_id=1, source_target_pairs={{0,3},{1,4},{2,5},{3,6},{4,7},{5,8},{6,9},{7,10},{8,11},{9,12},{10... | collective-permute-start | bytes 55304
  212.7 15.3 %collective-permute-start.3 = (bf16[16,576]{1,0:T(8,128)(2,1)S(1)}, bf16[16,576]{1,0:T(8,128)(2,1)S(1)}, u32[]{:S(2)}, u32[]{:S(2)}) collective-permute-start(bf16[16,576]{1,0:T(8,128)(2,1)S(1)} %convert.14), channel_id=1, source_target_pairs={{0,4},{1,5},{2,6},{3,7},{4,8},{5,9},{6,10},{7,11},{8,12},{9,13},{1... | collective-permute-start | bytes 55304
  217.6 10.4 %collective-permute-start.4 = (bf16[16,576]{1,0:T(8,128)(2,1)S(1)}, bf16[16,576]{1,0:T(8,128)(2,1)S(1)}, u32[]{:S(2)}, u32[]{:S(2)}) collective-permute-start(bf16[16,576]{1,0:T(8,128)(2,1)S(1)} %convert.14), channel_id=1, source_target_pairs={{0,5},{1,6},{2,7},{3,8},{4,9},{5,10},{6,11},{7,12},{8,13},{9,14},{... | collective-permute-start | bytes 55304
  219.8 8.3 %collective-permute-start.5 = (bf16[16,576]{1,0:T(8,128)(2,1)S(1)}, bf16[16,576]{1,0:T(8,128)(2,1)S(1)}, u32[]{:S(2)}, u32[]{:S(2)}) collective-permute-start(bf16[16,576]{1,0:T(8,128)(2,1)S(1)} %convert.14), channel_id=1, source_target_pairs={{0,6},{1,7},{2,8},{3,9},{4,10},{5,11},{6,12},{7,13},{8,14},{9,15},... | collective-permute-start | bytes 55304
  223.2 4.8 collective-permute-start.6
  229.4 230.8 %copy-start.2 = (bf16[256,1,576]{0,2,1:T(8,128)(2,1)S(1)}, bf16[256,1,576]{0,2,1:T(8,128)(2,1)}, u32[]{:S(2)}) copy-start(bf16[256,1,576]{0,2,1:T(8,128)(2,1)} %param.14) | copy-start | bytes 884740
  229.4 230.8 %copy-start.6 = (f32[256]{0:T(256)S(1)}, f32[256]{0:T(256)}, u32[]{:S(2)}) copy-start(f32[256]{0:T(256)} %param.13) | copy-start | bytes 3076
  280.2 269.0 %copy-start.7 = (f32[1,576]{1,0:T(1,128)S(1)}, f32[1,576]{1,0:T(1,128)}, u32[]{:S(2)}) copy-start(f32[1,576]{1,0:T(1,128)} %param.15) | copy-start | bytes 6916
  280.2 397.0 %all-reduce.10.cloned.1.call-start = ((), (), s32[]{:S(2)}) async-start(), calls=%async_computation.2 | async-start | bytes 786432 | tf_op jit(solution)/shard_map/psum | solution.py:64
  520.7 23.1 %collective-permute-start.10 = (f32[16,576]{1,0:T(8,128)S(1)}, f32[16,576]{1,0:T(8,128)S(1)}, u32[]{:S(2)}, u32[]{:S(2)}) collective-permute-start(f32[16,576]{1,0:T(8,128)S(1)} %fusion.1), channel_id=1, source_target_pairs={{0,3},{1,4},{2,5},{3,6},{4,7},{5,8},{6,9},{7,10},{8,11},{9,12},{10... | collective-permute-start | bytes 110600
  522.0 24.9 %collective-permute-start.11 = (f32[16,576]{1,0:T(8,128)S(1)}, f32[16,576]{1,0:T(8,128)S(1)}, u32[]{:S(2)}, u32[]{:S(2)}) collective-permute-start(f32[16,576]{1,0:T(8,128)S(1)} %fusion.1), channel_id=1, source_target_pairs={{0,4},{1,5},{2,6},{3,7},{4,8},{5,9},{6,10},{7,11},{8,12},{9,13},{1... | collective-permute-start | bytes 110600
  525.5 15.5 %collective-permute-start.15 = (f32[12,576]{1,0:T(8,128)S(1)}, f32[12,576]{1,0:T(8,128)S(1)}, u32[]{:S(2)}, u32[]{:S(2)}) collective-permute-start(f32[12,576]{1,0:T(8,128)S(1)} %slice.11), channel_id=1, source_target_pairs={{0,8},{1,9},{2,10},{3,11},{4,12},{5,13},{6,14},{7,15},{8,16},{9,17... | collective-permute-start | bytes 82952
  532.6 16.7 %collective-permute-start.12 = (f32[16,576]{1,0:T(8,128)S(1)}, f32[16,576]{1,0:T(8,128)S(1)}, u32[]{:S(2)}, u32[]{:S(2)}) collective-permute-start(f32[16,576]{1,0:T(8,128)S(1)} %fusion.1), channel_id=1, source_target_pairs={{0,5},{1,6},{2,7},{3,8},{4,9},{5,10},{6,11},{7,12},{8,13},{9,14},{... | collective-permute-start | bytes 110600
  537.1 12.2 %collective-permute-start.13 = (f32[16,576]{1,0:T(8,128)S(1)}, f32[16,576]{1,0:T(8,128)S(1)}, u32[]{:S(2)}, u32[]{:S(2)}) collective-permute-start(f32[16,576]{1,0:T(8,128)S(1)} %fusion.1), channel_id=1, source_target_pairs={{0,6},{1,7},{2,8},{3,9},{4,10},{5,11},{6,12},{7,13},{8,14},{9,15},... | collective-permute-start | bytes 110600
  541.0 8.2 %collective-permute-start.14 = (f32[16,576]{1,0:T(8,128)S(1)}, f32[16,576]{1,0:T(8,128)S(1)}, u32[]{:S(2)}, u32[]{:S(2)}) collective-permute-start(f32[16,576]{1,0:T(8,128)S(1)} %fusion.1), channel_id=1, source_target_pairs={{0,7},{1,8},{2,9},{3,10},{4,11},{5,12},{6,13},{7,14},{8,15},{9,16}... | collective-permute-start | bytes 110600
  543.9 5.4 collective-permute-start.8
  547.0 3.3 collective-permute-start.9
  551.3 126.5 %copy-start.1 = (f32[384,256]{1,0:T(8,128)S(1)}, f32[384,256]{1,0:T(8,128)}, u32[]{:S(2)}) copy-start(f32[384,256]{1,0:T(8,128)} %all-reduce.8.cloned.1.call-done) | copy-start | bytes 1179652
  601.5 151.6 %all-reduce.12.cloned.1.call-start = ((), (), s32[]{:S(2)}) async-start(), calls=%async_computation.3 | async-start | bytes 786432 | tf_op jit(solution)/shard_map/psum | solution.py:64
Sparse Core Ops, SparseCore 0:
  74.2 47.5 reduce-scatter.7
  280.3 179.8 all-reduce.7
  601.6 75.4 all-reduce.9
  679.3 73.7 all-reduce.11
